TPU v7x, 32 devices: a whole 2x2x4 slice. The times are simulated.
32 devices in a mesh: task: 16 (over z, y, x), shard: 2 (over core).
Axes of the slice: x: 2, y: 2, z: 4, core: 2. Of those that a mesh axis runs over, the one named last changes fastest.
Arguments:
- tokens: bfloat16 [16, 512, 1024], P('task'), may hold values from -6 to 6
- targets: bfloat16 [16, 512, 1024], P('task'), may hold values from -6 to 6
- meta_tokens: bfloat16 [16, 512, 1024], P('task'), may hold values from -6 to 6
- meta_targets: bfloat16 [16, 512, 1024], P('task'), may hold values from -6 to 6
- gate_weight: bfloat16 [16, 1024, 1536], P('task', None, 'shard'), may hold values from -0.1875 to 0.1875
- up_weight: bfloat16 [16, 1024, 1536], P('task', None, 'shard'), may hold values from -0.1875 to 0.1875
- down_weight: bfloat16 [16, 1536, 1024], P('task', 'shard'), may hold values from -0.15625 to 0.15625
- task_step: int32 [16], P('task'), may hold values from 0 to 9999
- hidden_state: float32 [16, 3, 512], P('task'), may hold values from -3 to 3
- cell_state: float32 [16, 3, 512], P('task'), may hold values from -6 to 6
- recurrent_weight: float32 [512, 2048], P('task'), may hold values from -0.25 to 0.25
- input_weight: float32 [3, 2048], replicated, may hold values from -3.5 to 3.5
- lstm_bias: float32 [2048], replicated, may hold values from -3 to 3
- context_weight: float32 [512, 5], replicated, may hold values from -0.25 to 0.25
- mlp_weight: float32 [3, 4], replicated, may hold values from -4 to 4
Outputs:
- gate_update: bfloat16 [16, 1024, 1536], P('task', None, 'shard')
- up_update: bfloat16 [16, 1024, 1536], P('task', None, 'shard')
- down_update: bfloat16 [16, 1536, 1024], P('task', 'shard')
- new_hidden: float32 [16, 3, 512], P('task')
- new_cell: float32 [16, 3, 512], P('task')
- meta_loss: float32 [], replicated
All inputs are finite; a program needn't handle non-finite values.
Results may differ from a plain program's by a relative error of at most 0.0056.
Values sent between devices are 32-bit elements; how exact they have to be, the bound alone decides.
A program may use at most 128 MiB of HBM per device.

v0:
```python
import jax
import jax.numpy as jnp
from jax import lax
from jax.sharding import PartitionSpec as P

STEPS = 10000
highest = lax.Precision.HIGHEST
epsilon = 1e-06
rate_factor = 0.1


def block_forward(inputs, w_gate, w_up, w_down):
    gate_pre = jnp.dot(inputs, w_gate, preferred_element_type=jnp.float32)
    up_pre = jnp.dot(inputs, w_up, preferred_element_type=jnp.float32)
    sigmoid_gate = jax.nn.sigmoid(gate_pre)
    activated = (gate_pre * sigmoid_gate * up_pre).astype(jnp.bfloat16)
    output = jnp.dot(activated, w_down, preferred_element_type=jnp.float32)
    return (gate_pre, up_pre, sigmoid_gate, activated, output)


def block_grads(inputs, w_down, gate_pre, up_pre, sigmoid_gate, activated, d_out):
    d_act = lax.dot_general(
        d_out, w_down, (((1,), (1,)), ((), ())), preferred_element_type=jnp.float32
    )
    d_gate = (d_act * up_pre * sigmoid_gate * (1.0 + gate_pre * (1.0 - sigmoid_gate))).astype(
        jnp.bfloat16
    )
    d_up = (d_act * gate_pre * sigmoid_gate).astype(jnp.bfloat16)
    grad_gate = lax.dot_general(
        inputs, d_gate, (((0,), (0,)), ((), ())), preferred_element_type=jnp.float32
    )
    grad_up = lax.dot_general(
        inputs, d_up, (((0,), (0,)), ((), ())), preferred_element_type=jnp.float32
    )
    grad_down = lax.dot_general(
        activated, d_out, (((0,), (0,)), ((), ())), preferred_element_type=jnp.float32
    )
    return (grad_gate, grad_up, grad_down)


def lstm_step(features, recurrent_term, cell_old, input_weight, lstm_bias, context_weight):
    state_width = cell_old.shape[-1]
    lstm_in = jnp.dot(features, input_weight, precision=highest) + recurrent_term + lstm_bias
    in_gate = jax.nn.sigmoid(lstm_in[:, :state_width])
    forget_gate = jax.nn.sigmoid(lstm_in[:, state_width : 2 * state_width])
    candidate = jnp.tanh(lstm_in[:, 2 * state_width : 3 * state_width])
    out_gate = jax.nn.sigmoid(lstm_in[:, 3 * state_width :])
    cell_new = forget_gate * cell_old + in_gate * candidate
    hidden_new = out_gate * jnp.tanh(cell_new)
    context = jnp.dot(hidden_new, context_weight, precision=highest)
    return (hidden_new, cell_new, context)


def param_update(param, gradient, rms_param, rms_grad, context_row, mlp_weight):
    p_norm = param.astype(jnp.float32) / rms_param
    g_norm = gradient / rms_grad
    summed = jnp.zeros(param.shape, jnp.float32)
    for hidden_unit in range(mlp_weight.shape[1]):
        inner = (
            mlp_weight[0, hidden_unit] * p_norm
            + mlp_weight[1, hidden_unit] * g_norm
            + context_row[hidden_unit]
        )
        summed = summed + mlp_weight[2, hidden_unit] * jax.nn.relu(inner)
    update = jnp.exp(context_row[-1]) * summed
    new_param = (param.astype(jnp.float32) - rate_factor * rms_param * update).astype(jnp.bfloat16)
    return (update.astype(jnp.bfloat16), new_param)


def local(
    tokens,
    targets,
    meta_tokens,
    meta_targets,
    gate_weight,
    up_weight,
    down_weight,
    task_step,
    hidden_state,
    cell_state,
    recurrent_weight,
    input_weight,
    lstm_bias,
    context_weight,
    mlp_weight,
):
    inputs = tokens[0]
    wanted = targets[0]
    meta_in = meta_tokens[0]
    meta_want = meta_targets[0]
    params = (gate_weight[0], up_weight[0], down_weight[0])
    gate_pre, up_pre, sigmoid_gate, activated, partial_out = block_forward(
        inputs, params[0], params[1], params[2]
    )
    output = lax.psum(partial_out, "shard")
    d_out = (output - wanted.astype(jnp.float32)).astype(jnp.bfloat16)
    gradients = block_grads(inputs, params[2], gate_pre, up_pre, sigmoid_gate, activated, d_out)
    grad_sq = jnp.stack([jnp.sum(grad_piece * grad_piece) for grad_piece in gradients])
    param_sq = jnp.stack(
        [jnp.sum(jnp.square(param_piece.astype(jnp.float32))) for param_piece in params]
    )
    tensor_sums = lax.psum(jnp.stack([grad_sq, param_sq]), "shard")
    entries = float(params[0].size * lax.axis_size("shard"))
    rms_grad = jnp.sqrt(tensor_sums[0] / entries + epsilon)
    rms_param = jnp.sqrt(tensor_sums[1] / entries + epsilon)
    fraction = jnp.full((3,), task_step[0].astype(jnp.float32) / STEPS, jnp.float32)
    features = jnp.stack([jnp.log(rms_grad), jnp.log(rms_param), fraction], axis=1)
    hidden_old = hidden_state[0]
    recurrent_term = jnp.dot(
        hidden_old, lax.all_gather(recurrent_weight, "task", axis=0, tiled=True), precision=highest
    )
    hidden_new, cell_new, context = lstm_step(
        features, recurrent_term, cell_state[0], input_weight, lstm_bias, context_weight
    )
    results = [
        param_update(
            params[tensor_id],
            gradients[tensor_id],
            rms_param[tensor_id],
            rms_grad[tensor_id],
            context[tensor_id],
            mlp_weight,
        )
        for tensor_id in range(3)
    ]
    meta_partial = block_forward(meta_in, results[0][1], results[1][1], results[2][1])[4]
    loss_scale = 0.5 / (meta_want.shape[0] * meta_want.shape[1])
    meta_share = lax.psum_scatter(meta_partial, "shard", scatter_dimension=1, tiled=True)
    share_cols = meta_share.shape[1]
    want_share = lax.dynamic_slice_in_dim(
        meta_want, lax.axis_index("shard") * share_cols, share_cols, 1
    )
    meta_part = loss_scale * jnp.sum(jnp.square(meta_share - want_share.astype(jnp.float32)))
    summed = lax.psum(meta_part, ("task", "shard"))
    meta_loss = summed / lax.axis_size("task")
    return (
        results[0][0][None],
        results[1][0][None],
        results[2][0][None],
        hidden_new[None],
        cell_new[None],
        meta_loss,
    )


def solution(mesh):
    return jax.shard_map(
        local,
        mesh=mesh,
        in_specs=(
            P("task", None, None),
            P("task", None, None),
            P("task", None, None),
            P("task", None, None),
            P("task", None, "shard"),
            P("task", None, "shard"),
            P("task", "shard", None),
            P("task"),
            P("task", None, None),
            P("task", None, None),
            P("task", None),
            P(),
            P(),
            P(),
            P(),
        ),
        out_specs=(
            P("task", None, "shard"),
            P("task", None, "shard"),
            P("task", "shard", None),
            P("task", None, None),
            P("task", None, None),
            P(),
        ),
        check_vma=False,
    )
```

profile of v0, /device:TPU:0, one launch (start us, length us, event | category | flops | bytes accessed | tf_op | source)
XLA Modules:
  0.0 225.3 jit_solution(7514482021820399542)
XLA Ops:
  9.2 2.4 %fusion.48 = f32[512,768]{1,0:T(8,128)S(1)} fusion(bf16[1,1024,768]{2,1,0:T(8,128)(2,1)} %param.19, bf16[1,512,1024]{2,1,0:T(8,128)(2,1)S(1)} %copy-done), kind=kOutput, calls=%fused_computation.68 | convolution fusion | flops 805306368 | bytes 4194304 | tf_op jit(solution)/shard_map/dot_general | solution.py:13
  11.7 2.1 multiply_convert_fusion.2
  13.8 2.3 %fusion.57 = f32[512,1024]{1,0:T(8,128)} fusion(bf16[512,768]{1,0:T(8,128)(2,1)S(1)} %get-tuple-element.57, bf16[1,768,1024]{2,1,0:T(8,128)(2,1)S(1)} %copy-done.4), kind=kOutput, calls=%fused_computation.80 | convolution fusion | flops 805306368 | bytes 4456448 | tf_op jit(solution)/shard_map/dot_general | solution.py:17
  16.8 1.7 copy.22
  18.5 2.6 %copy.21 = bf16[1,1024,768]{1,2,0:T(8,128)(2,1)} copy(bf16[1,1024,768]{2,1,0:T(8,128)(2,1)} %param.19) | data formatting | bytes 3145728 | tf_op args[4]
  22.6 2.8 %fusion.4 = f32[]{:T(128)} fusion(bf16[1,768,1024]{2,1,0:T(8,128)(2,1)} %param.21), kind=kLoop, calls=%fused_computation.13 | loop fusion | flops 2359295 | bytes 1572868 | tf_op jit(solution)/shard_map/reduce_sum | solution.py:100
  28.3 12.0 %all-reduce.2.cloned.1.call-done = f32[512,1024]{1,0:T(8,128)} async-done(((f32[512,1024]{1,0:T(8,128)}), f32[512,1024]{1,0:T(8,128)}) %all-reduce.2.cloned.1.call-update) | async-done | bytes 2097168 | tf_op jit(solution)/shard_map/psum | solution.py:95
  40.3 3.5 %fusion.55 = f32[512,768]{1,0:T(8,128)S(1)} fusion(bf16[1,768,1024]{2,1,0:T(8,128)(2,1)} %param.21, f32[512,1024]{1,0:T(8,128)} %all-reduce.2.cloned.1.call-done, bf16[1,512,1024]{2,1,0:T(8,128)(2,1)} %param.16), kind=kOutput, calls=%fused_computation.78 | convolution fusion | flops 806879232 | bytes 6291456 | tf_op jit(solution)/shard_map/dot_general | solution.py:22
  43.9 3.3 %multiply_reduce_fusion = (f32[]{:T(128)}, f32[768,1024]{1,0:T(8,128)}) fusion(bf16[512,768]{1,0:T(8,128)(2,1)S(1)} %get-tuple-element.57, f32[512,1024]{1,0:T(8,128)S(1)} %copy-done.6, bf16[1,512,1024]{2,1,0:T(8,128)(2,1)S(1)} %copy-done.8), kind=kOutput, calls=%fused_computation.56 | convolution fusion | flops 808452096 | bytes 7077892 | tf_op jit(solution)/shard_map/dot_general | solution.py:35
  47.3 3.5 %multiply_reduce_fusion.1 = (f32[]{:T(128)}, f32[768,1024]{1,0:T(8,128)}) fusion(bf16[1,512,1024]{2,1,0:T(8,128)(2,1)S(1)} %copy-done, f32[512,768]{1,0:T(8,128)S(1)} %fusion.55, f32[512,768]{1,0:T(8,128)S(1)} %copy-done.21), kind=kOutput, calls=%fused_computation.57 | convolution fusion | flops 809238528 | bytes 7340036 | tf_op jit(solution)/shard_map/dot_general | solution.py:32
  50.7 3.6 %multiply_reduce_fusion.2 = (f32[]{:T(128)}, f32[768,1024]{1,0:T(8,128)}) fusion(bf16[1,512,1024]{2,1,0:T(8,128)(2,1)S(1)} %copy-done, f32[512,768]{1,0:T(8,128)S(1)} %copy-done.21, f32[512,768]{1,0:T(8,128)S(1)} %fusion.55, f32[512,768]{1,0:T(8,128)S(1)} %copy-done.22), kind=kOutput, calls=%fused_computation.58 | convolution fusion | flops 810811392 | bytes 8912900 | tf_op jit(solution)/shard_map/dot_general | solution.py:29
  54.3 3.9 %maximum_bitcast_fusion = (f32[1,3]{1,0:T(1,128)S(1)}, f32[1,3]{1,0:T(1,128)S(1)}) fusion(f32[1]{0:T(128)} %bitcast.7, f32[1]{0:T(128)} %bitcast.6, f32[1]{0:T(128)} %bitcast.5, f32[1]{0:T(128)} %bitcast.11, f32[1]{0:T(128)} %bitcast.10, f32[1]{0:T(128)} %bitcast.9), kind=kLoop, calls=%fused_computation.130 | loop fusion | flops 12 | bytes 48 | tf_op jit(solution)/shard_map/stack | solution.py:102
  58.3 2.6 %psum.22 = f32[2,3]{1,0:T(2,128)S(1)} all-reduce(f32[2,3]{1,0:T(2,128)S(1)} %pad_maximum_fusion), channel_id=1, replica_groups=mesh['task'=16,'shard'=2] {'shard'}, use_global_device_ids=true, to_apply=%region_7.0 | all-reduce | flops 6 | bytes 48 | tf_op jit(solution)/shard_map/psum | solution.py:102
  64.3 33.4 %all-gather.2.cloned.1.call-done = f32[512,2048]{1,0:T(8,128)} async-done(((f32[32,2048]{1,0:T(8,128)}), f32[512,2048]{1,0:T(8,128)}) %all-gather.2.cloned.1.call-update) | async-done | bytes 4194320 | tf_op jit(solution)/shard_map/all_gather | solution.py:110
  97.7 4.4 %fusion.38 = f32[3,2048]{1,0:T(4,128)S(1)} fusion(f32[3,2048]{1,0:T(4,128)S(1)} %fusion.93, f32[512,2048]{1,0:T(8,128)} %all-gather.2.cloned.1.call-done, f32[2048]{0:T(1024)S(1)} %copy-done.18, f32[1,3,512]{2,0,1:T(1,128)S(1)} %copy-done.17), kind=kOutput, calls=%fused_computation.60 | convolution fusion | flops 37761024 | bytes 4257792 | tf_op jit(solution)/shard_map/dot_general | solution.py:109
  105.0 15.6 %convert_bitcast_fusion.1 = (bf16[1,1024,768]{1,2,0:T(8,128)(2,1)}, f32[1024,768]{0,1:T(8,128)S(1)}) fusion(f32[]{:T(128)} %bitcast.50, f32[]{:T(128)} %bitcast.36, f32[]{:T(128)} %bitcast.35, f32[]{:T(128)} %bitcast.34, f32[]{:T(128)} %bitcast.48, f32[]{:T(128)} %bitcast.31, f32[]{:T(128)} %bitcast.30, f32[]{:T(128)} %bitcast.29, f32[]{:T(128)} %bitcast.46, ...), kind=kLoop, calls=%fused_computation.88 | loop fusion | flops 25165824 | bytes 9437260 | tf_op jit(solution)/shard_map/broadcast_in_dim | solution.py:138
  120.6 2.3 %fusion.42 = f32[768,512]{0,1:T(8,128)} fusion(f32[1024,768]{0,1:T(8,128)S(1)} %get-tuple-element.15, bf16[1,1024,768]{1,2,0:T(8,128)(2,1)S(1)} %copy.22, f32[]{:T(128)S(6)} %mul.394, bf16[1,512,1024]{2,1,0:T(8,128)(2,1)S(1)} %copy-done.12), kind=kOutput, calls=%fused_computation.64 | convolution fusion | flops 808452096 | bytes 7340036 | tf_op jit(solution)/shard_map/dot_general | solution.py:14
  123.5 16.5 %convert_bitcast_fusion = (bf16[1,768,1024]{2,1,0:T(8,128)(2,1)}, f32[768,1024]{1,0:T(8,128)}) fusion(f32[]{:T(128)} %bitcast.58, f32[]{:T(128)} %bitcast.36, f32[]{:T(128)} %bitcast.35, f32[]{:T(128)} %bitcast.34, f32[]{:T(128)} %bitcast.57, f32[]{:T(128)} %bitcast.31, f32[]{:T(128)} %bitcast.30, f32[]{:T(128)} %bitcast.29, f32[]{:T(128)} %bitcast.56, ...), kind=kLoop, calls=%fused_computation.87 | loop fusion | flops 25165824 | bytes 9437260 | tf_op jit(solution)/shard_map/broadcast_in_dim | solution.py:139
  140.1 16.0 %convert_bitcast_fusion.2 = (bf16[1,1024,768]{1,2,0:T(8,128)(2,1)}, f32[1024,768]{0,1:T(8,128)}) fusion(f32[]{:T(128)} %bitcast.38, f32[]{:T(128)} %bitcast.36, f32[]{:T(128)} %bitcast.35, f32[]{:T(128)} %bitcast.34, f32[]{:T(128)} %bitcast.33, f32[]{:T(128)} %bitcast.31, f32[]{:T(128)} %bitcast.30, f32[]{:T(128)} %bitcast.29, f32[]{:T(128)} %bitcast.28, ...), kind=kLoop, calls=%fused_computation.89 | loop fusion | flops 25165824 | bytes 9437260 | tf_op jit(solution)/shard_map/broadcast_in_dim | solution.py:137
  156.1 7.8 %fusion.40 = f32[512,1024]{1,0:T(8,128)} fusion(f32[768,1024]{1,0:T(8,128)} %get-tuple-element.13, bf16[1,768,1024]{2,1,0:T(8,128)(2,1)} %param.21, f32[]{:T(128)S(6)} %mul.398, f32[768,512]{0,1:T(8,128)} %fusion.42, bf16[1,512,1024]{2,1,0:T(8,128)(2,1)} %param.17, f32[1024,768]{0,1:T(8,128)} %get-tuple-element.17, bf16[1,1024,768]{1,2,0:T(8,128)(2,1)S(1)} %copy-done.3, ...), kind=kOutput, calls=%fused_computation.63 | convolution fusion | flops 1619263488 | bytes 14155784 | tf_op jit(solution)/shard_map/dot_general | solution.py:17
  166.8 2.7 %copy.24 = bf16[1,1024,768]{2,1,0:T(8,128)(2,1)} copy(bf16[1,1024,768]{1,2,0:T(8,128)(2,1)} %get-tuple-element.16) | data formatting | bytes 3145728
  170.1 2.2 reduce-scatter.2.cloned.1.call-done
  172.3 2.1 fusion.65
  175.6 40.5 %psum.23 = f32[]{:T(128)} all-reduce(f32[]{:T(128)S(6)} %mul_shard_map.3), channel_id=1, replica_groups=mesh['task'=16,'shard'=2] {'task','shard'}, use_global_device_ids=true, to_apply=%region_10.11 | all-reduce | flops 1 | bytes 8 | tf_op jit(solution)/shard_map/psum | solution.py:134
  (67 shorter events, 12.9 us)
Async XLA Ops:
  8.0 3.6 %copy-start.11 = (bf16[1,1024,768]{2,1,0:T(8,128)(2,1)S(1)}, bf16[1,1024,768]{2,1,0:T(8,128)(2,1)}, u32[]{:S(2)}) copy-start(bf16[1,1024,768]{2,1,0:T(8,128)(2,1)} %param.20) | copy-start | bytes 4718596
  8.0 32.3 %all-reduce.2.cloned.1.call-start = ((), (), s32[]{:S(2)}) async-start(), calls=%async_computation.1 | async-start | bytes 4194304 | tf_op jit(solution)/shard_map/psum | solution.py:95
  11.6 2.2 copy-start.20
  11.6 2.2 copy-start.4
  16.2 81.5 %all-gather.2.cloned.1.call-start = ((), (), s32[]{:S(2)}) async-start(), calls=%async_computation.2 | async-start | bytes 4456448 | tf_op jit(solution)/shard_map/all_gather | solution.py:110
  16.7 5.1 %copy-start.15 = (f32[3,4]{1,0:T(4,128)S(1)}, f32[3,4]{1,0:T(4,128)}, u32[]{:S(2)}) copy-start(f32[3,4]{1,0:T(4,128)} %param.29) | copy-start | bytes 148
  16.8 155.5 %reduce-scatter.2.cloned.1.call-start = ((), (), s32[]{:S(2)}) async-start(), calls=%async_computation.3 | async-start | bytes 3145728 | tf_op jit(solution)/shard_map/reduce_scatter | solution.py:128
  21.1 5.7 %copy-start.2 = (bf16[1,1024,768]{1,2,0:T(8,128)(2,1)S(1)}, bf16[1,1024,768]{1,2,0:T(8,128)(2,1)}, u32[]{:S(2)}) copy-start(bf16[1,1024,768]{1,2,0:T(8,128)(2,1)} %copy.21) | copy-start | bytes 4718596
  40.3 3.5 %copy-start.6 = (f32[512,1024]{1,0:T(8,128)S(1)}, f32[512,1024]{1,0:T(8,128)}, u32[]{:S(2)}) copy-start(f32[512,1024]{1,0:T(8,128)} %all-reduce.2.cloned.1.call-done) | copy-start | bytes 6291460
  40.3 3.5 %copy-start.8 = (bf16[1,512,1024]{2,1,0:T(8,128)(2,1)S(1)}, bf16[1,512,1024]{2,1,0:T(8,128)(2,1)}, u32[]{:S(2)}) copy-start(bf16[1,512,1024]{2,1,0:T(8,128)(2,1)} %param.16) | copy-start | bytes 3145732
  43.9 3.4 %copy-start.21 = (f32[512,768]{1,0:T(8,128)S(1)}, f32[512,768]{1,0:T(8,128)}, u32[]{:S(2)}) copy-start(f32[512,768]{1,0:T(8,128)} %copy-done.20) | copy-start | bytes 4718596
  47.3 3.5 %copy-start.22 = (f32[512,768]{1,0:T(8,128)S(1)}, f32[512,768]{1,0:T(8,128)}, u32[]{:S(2)}) copy-start(f32[512,768]{1,0:T(8,128)} %get-tuple-element.58) | copy-start | bytes 4718596
  50.7 13.3 %copy-start.14 = (f32[3,2048]{1,0:T(4,128)S(1)}, f32[3,2048]{1,0:T(4,128)}, u32[]{:S(2)}) copy-start(f32[3,2048]{1,0:T(4,128)} %param.26) | copy-start | bytes 73732
  50.7 46.9 %copy-start.17 = (f32[1,3,512]{2,0,1:T(1,128)S(1)}, f32[1,3,512]{2,0,1:T(1,128)}, u32[]{:S(2)}) copy-start(f32[1,3,512]{2,0,1:T(1,128)} %param.23) | copy-start | bytes 18436
  50.7 46.9 %copy-start.18 = (f32[2048]{0:T(1024)S(1)}, f32[2048]{0:T(1024)}, u32[]{:S(2)}) copy-start(f32[2048]{0:T(1024)} %param.27) | copy-start | bytes 24580
  54.3 47.7 %copy-start.19 = (f32[1,3,512]{2,0,1:T(1,128)S(1)}, f32[1,3,512]{2,0,1:T(1,128)}, u32[]{:S(2)}) copy-start(f32[1,3,512]{2,0,1:T(1,128)} %param.24) | copy-start | bytes 18436
  54.3 47.8 %copy-start.16 = (f32[512,5]{0,1:T(8,128)S(1)}, f32[512,5]{0,1:T(8,128)}, u32[]{:S(2)}) copy-start(f32[512,5]{0,1:T(8,128)} %param.28) | copy-start | bytes 30724
  97.7 7.3 %copy-start.10 = (f32[768,1024]{1,0:T(8,128)S(1)}, f32[768,1024]{1,0:T(8,128)}, u32[]{:S(2)}) copy-start(f32[768,1024]{1,0:T(8,128)} %get-tuple-element.62) | copy-start | bytes 9437188
  105.0 15.6 %copy-start.12 = (bf16[1,512,1024]{2,1,0:T(8,128)(2,1)S(1)}, bf16[1,512,1024]{2,1,0:T(8,128)(2,1)}, u32[]{:S(2)}) copy-start(bf16[1,512,1024]{2,1,0:T(8,128)(2,1)} %param.17) | copy-start | bytes 3145732
  120.6 2.3 %copy-start.1 = (f32[768,1024]{1,0:T(8,128)S(1)}, f32[768,1024]{1,0:T(8,128)}, u32[]{:S(2)}) copy-start(f32[768,1024]{1,0:T(8,128)} %get-tuple-element.60) | copy-start | bytes 9437188
  120.6 2.9 %copy-start.5 = (bf16[1,768,1024]{2,1,0:T(8,128)(2,1)S(1)}, bf16[1,768,1024]{2,1,0:T(8,128)(2,1)}, u32[]{:S(2)}) copy-start(bf16[1,768,1024]{2,1,0:T(8,128)(2,1)} %param.21) | copy-start | bytes 4718596
  123.5 16.6 %copy-start.3 = (bf16[1,1024,768]{1,2,0:T(8,128)(2,1)S(1)}, bf16[1,1024,768]{1,2,0:T(8,128)(2,1)}, u32[]{:S(2)}) copy-start(bf16[1,1024,768]{1,2,0:T(8,128)(2,1)} %copy.21) | copy-start | bytes 4718596
  123.5 16.6 %copy-start.9 = (f32[768,1024]{1,0:T(8,128)S(1)}, f32[768,1024]{1,0:T(8,128)}, u32[]{:S(2)}) copy-start(f32[768,1024]{1,0:T(8,128)} %get-tuple-element.64) | copy-start | bytes 9437188
  166.8 5.4 %copy-start.13 = (bf16[1,512,1024]{2,1,0:T(8,128)(2,1)S(1)}, bf16[1,512,1024]{2,1,0:T(8,128)(2,1)}, u32[]{:S(2)}) copy-start(bf16[1,512,1024]{2,1,0:T(8,128)(2,1)} %param.18) | copy-start | bytes 3145732
  (2 other events, 2.6 us)
Sparse Core Ops, SparseCore 0:
  16.3 24.0 all-reduce.1
  164.0 8.2 reduce-scatter.1
Sparse Core Ops, SparseCore 1:
  19.4 78.2 all-gather.1
where the time goes:
time: 226 us; the launch traced here: 225 us
  other arithmetic  59.9 us (27%)
  waiting for transfers between devices  48.1 us (21%)
  blocking collectives  43.1 us (19%)
  matrix products  35.7 us (16%)
  between operations  22.6 us (10%)
  local copies, waits for them, and re-layouts  15.8 us (7%)
    psum x1, blocking collectives, local(): summed = lax.psum(meta_part, ('task', 'shard'))  40.5 us
    all_gather x1, waiting for transfers between devices, local(): lax.all_gather(recurrent_weight, 'task', axis=0, tiled=True)  33.4 us
    broadcast_in_dim x1, other arithmetic, local(): results[2][0][None]  16.5 us
    broadcast_in_dim x1, other arithmetic, local(): results[0][0][None]  16 us
    broadcast_in_dim x1, other arithmetic, local(): results[1][0][None]  15.6 us
    unnamed x52, local copies, waits for them, and re-layouts  13 us
    psum x1, waiting for transfers between devices, local(): output = lax.psum(partial_out, 'shard')  12 us
    dot_general x2, matrix products, block_forward(): output = jnp.dot(activated, w_down, preferred_element_type=jnp.float32)  10.1 us
  transfers between devices with their start and end apart: 3, of which 3 were waited for; matrix products, arithmetic and copies ran while one was open for 16% of the time, Pallas kernels for 0%

commit v1 on v0

--- a/solution.py
+++ b/solution.py
@@ -131,7 +131,9 @@
         meta_want, lax.axis_index("shard") * share_cols, share_cols, 1
     )
     meta_part = loss_scale * jnp.sum(jnp.square(meta_share - want_share.astype(jnp.float32)))
-    summed = lax.psum(meta_part, ("task", "shard"))
+    summed = meta_part
+    for mesh_axis in ("shard", "task"):
+        summed = lax.psum(summed, mesh_axis)
     meta_loss = summed / lax.axis_size("task")
     return (
         results[0][0][None],

time: 226 us -> 232 us (1.027)
  blocking collectives: 43.1 us -> 48.3 us
    psum x1 -> x2, blocking collectives: 40.5 us -> 45.6 us  [local(): summed = lax.psum(summed, mesh_axis)]
  transfers between devices with their start and end apart: 3 -> 3, of which waited for: 3 -> 3; matrix products, arithmetic and copies ran while one was open for 16% -> 15% of each run, Pallas kernels for 0% -> 0%
where the time goes in v1:
time: 232 us; the launch traced here: 231 us
  other arithmetic  59.7 us (26%)
  blocking collectives  48.3 us (21%)
  waiting for transfers between devices  48.2 us (21%)
  matrix products  35.7 us (15%)
  between operations  22.8 us (10%)
  local copies, waits for them, and re-layouts  15.9 us (7%)
    psum x2, blocking collectives, local(): summed = lax.psum(summed, mesh_axis)  45.6 us
    all_gather x1, waiting for transfers between devices, local(): lax.all_gather(recurrent_weight, 'task', axis=0, tiled=True)  33 us
    broadcast_in_dim x1, other arithmetic, local(): results[2][0][None]  16.4 us
    broadcast_in_dim x1, other arithmetic, local(): results[0][0][None]  16 us
    broadcast_in_dim x1, other arithmetic, local(): results[1][0][None]  15.3 us
    unnamed x52, local copies, waits for them, and re-layouts  13 us
    psum x1, waiting for transfers between devices, local(): output = lax.psum(partial_out, 'shard')  11.9 us
    dot_general x2, matrix products, block_forward(): output = jnp.dot(activated, w_down, preferred_element_type=jnp.float32)  10.1 us
  transfers between devices with their start and end apart: 3, of which 3 were waited for; matrix products, arithmetic and copies ran while one was open for 15% of the time, Pallas kernels for 0%

profile of v1, /device:TPU:0, one launch (start us, length us, event | category | flops | bytes accessed | tf_op | source)
XLA Modules:
  0.0 230.7 jit_solution(17627008472409063550)
XLA Ops:
  9.2 2.4 %fusion.48 = f32[512,768]{1,0:T(8,128)S(1)} fusion(bf16[1,1024,768]{2,1,0:T(8,128)(2,1)} %param.19, bf16[1,512,1024]{2,1,0:T(8,128)(2,1)S(1)} %copy-done), kind=kOutput, calls=%fused_computation.68 | convolution fusion | flops 805306368 | bytes 4194304 | tf_op jit(solution)/shard_map/dot_general | solution.py:13
  11.7 2.1 multiply_convert_fusion.2
  13.8 2.3 %fusion.57 = f32[512,1024]{1,0:T(8,128)} fusion(bf16[512,768]{1,0:T(8,128)(2,1)S(1)} %get-tuple-element.57, bf16[1,768,1024]{2,1,0:T(8,128)(2,1)S(1)} %copy-done.4), kind=kOutput, calls=%fused_computation.80 | convolution fusion | flops 805306368 | bytes 4456448 | tf_op jit(solution)/shard_map/dot_general | solution.py:17
  18.5 2.6 %copy.21 = bf16[1,1024,768]{1,2,0:T(8,128)(2,1)} copy(bf16[1,1024,768]{2,1,0:T(8,128)(2,1)} %param.19) | data formatting | bytes 3145728 | tf_op args[4]
  22.6 2.9 %fusion.4 = f32[]{:T(128)} fusion(bf16[1,768,1024]{2,1,0:T(8,128)(2,1)} %param.21), kind=kLoop, calls=%fused_computation.13 | loop fusion | flops 2359295 | bytes 1572868 | tf_op jit(solution)/shard_map/reduce_sum | solution.py:100
  28.5 11.9 %all-reduce.2.cloned.1.call-done = f32[512,1024]{1,0:T(8,128)} async-done(((f32[512,1024]{1,0:T(8,128)}), f32[512,1024]{1,0:T(8,128)}) %all-reduce.2.cloned.1.call-update) | async-done | bytes 2097168 | tf_op jit(solution)/shard_map/psum | solution.py:95
  40.3 3.5 %fusion.55 = f32[512,768]{1,0:T(8,128)S(1)} fusion(bf16[1,768,1024]{2,1,0:T(8,128)(2,1)} %param.21, f32[512,1024]{1,0:T(8,128)} %all-reduce.2.cloned.1.call-done, bf16[1,512,1024]{2,1,0:T(8,128)(2,1)} %param.16), kind=kOutput, calls=%fused_computation.78 | convolution fusion | flops 806879232 | bytes 6291456 | tf_op jit(solution)/shard_map/dot_general | solution.py:22
  43.9 3.3 %multiply_reduce_fusion = (f32[]{:T(128)}, f32[768,1024]{1,0:T(8,128)}) fusion(bf16[512,768]{1,0:T(8,128)(2,1)S(1)} %get-tuple-element.57, f32[512,1024]{1,0:T(8,128)S(1)} %copy-done.6, bf16[1,512,1024]{2,1,0:T(8,128)(2,1)S(1)} %copy-done.8), kind=kOutput, calls=%fused_computation.56 | convolution fusion | flops 808452096 | bytes 7077892 | tf_op jit(solution)/shard_map/dot_general | solution.py:35
  47.3 3.4 %multiply_reduce_fusion.1 = (f32[]{:T(128)}, f32[768,1024]{1,0:T(8,128)}) fusion(bf16[1,512,1024]{2,1,0:T(8,128)(2,1)S(1)} %copy-done, f32[512,768]{1,0:T(8,128)S(1)} %fusion.55, f32[512,768]{1,0:T(8,128)S(1)} %copy-done.21), kind=kOutput, calls=%fused_computation.57 | convolution fusion | flops 809238528 | bytes 7340036 | tf_op jit(solution)/shard_map/dot_general | solution.py:32
  50.7 3.6 %multiply_reduce_fusion.2 = (f32[]{:T(128)}, f32[768,1024]{1,0:T(8,128)}) fusion(bf16[1,512,1024]{2,1,0:T(8,128)(2,1)S(1)} %copy-done, f32[512,768]{1,0:T(8,128)S(1)} %copy-done.21, f32[512,768]{1,0:T(8,128)S(1)} %fusion.55, f32[512,768]{1,0:T(8,128)S(1)} %copy-done.22), kind=kOutput, calls=%fused_computation.58 | convolution fusion | flops 810811392 | bytes 8912900 | tf_op jit(solution)/shard_map/dot_general | solution.py:29
  54.3 4.0 %maximum_bitcast_fusion = (f32[1,3]{1,0:T(1,128)S(1)}, f32[1,3]{1,0:T(1,128)S(1)}) fusion(f32[1]{0:T(128)} %bitcast.7, f32[1]{0:T(128)} %bitcast.6, f32[1]{0:T(128)} %bitcast.5, f32[1]{0:T(128)} %bitcast.11, f32[1]{0:T(128)} %bitcast.10, f32[1]{0:T(128)} %bitcast.9), kind=kLoop, calls=%fused_computation.130 | loop fusion | flops 12 | bytes 48 | tf_op jit(solution)/shard_map/stack | solution.py:102
  58.4 2.6 %psum.29 = f32[2,3]{1,0:T(2,128)S(1)} all-reduce(f32[2,3]{1,0:T(2,128)S(1)} %pad_maximum_fusion), channel_id=1, replica_groups=mesh['task'=16,'shard'=2] {'shard'}, use_global_device_ids=true, to_apply=%region_7.0 | all-reduce | flops 6 | bytes 48 | tf_op jit(solution)/shard_map/psum | solution.py:102
  64.6 33.0 %all-gather.2.cloned.1.call-done = f32[512,2048]{1,0:T(8,128)} async-done(((f32[32,2048]{1,0:T(8,128)}), f32[512,2048]{1,0:T(8,128)}) %all-gather.2.cloned.1.call-update) | async-done | bytes 4194320 | tf_op jit(solution)/shard_map/all_gather | solution.py:110
  97.6 4.4 %fusion.38 = f32[3,2048]{1,0:T(4,128)S(1)} fusion(f32[3,2048]{1,0:T(4,128)S(1)} %fusion.93, f32[512,2048]{1,0:T(8,128)} %all-gather.2.cloned.1.call-done, f32[2048]{0:T(1024)S(1)} %copy-done.18, f32[1,3,512]{2,0,1:T(1,128)S(1)} %copy-done.17), kind=kOutput, calls=%fused_computation.60 | convolution fusion | flops 37761024 | bytes 4257792 | tf_op jit(solution)/shard_map/dot_general | solution.py:109
  105.1 15.3 %convert_bitcast_fusion.1 = (bf16[1,1024,768]{1,2,0:T(8,128)(2,1)}, f32[1024,768]{0,1:T(8,128)S(1)}) fusion(f32[]{:T(128)} %bitcast.50, f32[]{:T(128)} %bitcast.36, f32[]{:T(128)} %bitcast.35, f32[]{:T(128)} %bitcast.34, f32[]{:T(128)} %bitcast.48, f32[]{:T(128)} %bitcast.31, f32[]{:T(128)} %bitcast.30, f32[]{:T(128)} %bitcast.29, f32[]{:T(128)} %bitcast.46, ...), kind=kLoop, calls=%fused_computation.88 | loop fusion | flops 25165824 | bytes 9437260 | tf_op jit(solution)/shard_map/broadcast_in_dim | solution.py:140
  120.4 2.3 fusion.42
  123.3 16.4 %convert_bitcast_fusion = (bf16[1,768,1024]{2,1,0:T(8,128)(2,1)}, f32[768,1024]{1,0:T(8,128)}) fusion(f32[]{:T(128)} %bitcast.58, f32[]{:T(128)} %bitcast.36, f32[]{:T(128)} %bitcast.35, f32[]{:T(128)} %bitcast.34, f32[]{:T(128)} %bitcast.57, f32[]{:T(128)} %bitcast.31, f32[]{:T(128)} %bitcast.30, f32[]{:T(128)} %bitcast.29, f32[]{:T(128)} %bitcast.56, ...), kind=kLoop, calls=%fused_computation.87 | loop fusion | flops 25165824 | bytes 9437260 | tf_op jit(solution)/shard_map/broadcast_in_dim | solution.py:141
  139.7 16.0 %convert_bitcast_fusion.2 = (bf16[1,1024,768]{1,2,0:T(8,128)(2,1)}, f32[1024,768]{0,1:T(8,128)}) fusion(f32[]{:T(128)} %bitcast.38, f32[]{:T(128)} %bitcast.36, f32[]{:T(128)} %bitcast.35, f32[]{:T(128)} %bitcast.34, f32[]{:T(128)} %bitcast.33, f32[]{:T(128)} %bitcast.31, f32[]{:T(128)} %bitcast.30, f32[]{:T(128)} %bitcast.29, f32[]{:T(128)} %bitcast.28, ...), kind=kLoop, calls=%fused_computation.89 | loop fusion | flops 25165824 | bytes 9437260 | tf_op jit(solution)/shard_map/broadcast_in_dim | solution.py:139
  155.7 7.8 %fusion.40 = f32[512,1024]{1,0:T(8,128)} fusion(f32[768,1024]{1,0:T(8,128)} %get-tuple-element.13, bf16[1,768,1024]{2,1,0:T(8,128)(2,1)} %param.21, f32[]{:T(128)S(6)} %mul.398, f32[768,512]{0,1:T(8,128)} %fusion.42, bf16[1,512,1024]{2,1,0:T(8,128)(2,1)} %param.17, f32[1024,768]{0,1:T(8,128)} %get-tuple-element.17, bf16[1,1024,768]{1,2,0:T(8,128)(2,1)S(1)} %copy-done.3, ...), kind=kOutput, calls=%fused_computation.63 | convolution fusion | flops 1619263488 | bytes 14155784 | tf_op jit(solution)/shard_map/dot_general | solution.py:17
  166.5 2.7 %copy.24 = bf16[1,1024,768]{2,1,0:T(8,128)(2,1)} copy(bf16[1,1024,768]{1,2,0:T(8,128)(2,1)} %get-tuple-element.16) | data formatting | bytes 3145728
  169.1 2.8 %reduce-scatter.2.cloned.1.call-done = f32[512,512]{1,0:T(8,128)} async-done(((f32[512,1024]{1,0:T(8,128)}), f32[512,512]{1,0:T(8,128)}) %reduce-scatter.2.cloned.1.call-update) | async-done | bytes 1048592 | tf_op jit(solution)/shard_map/reduce_scatter | solution.py:128
  171.9 2.1 fusion.65
  175.3 3.0 %psum.30 = f32[]{:T(128)} all-reduce(f32[]{:T(128)S(6)} %mul_shard_map.3), channel_id=1, replica_groups=mesh['task'=16,'shard'=2] {'shard'}, use_global_device_ids=true, to_apply=%region_10.11 | all-reduce | flops 1 | bytes 8 | tf_op jit(solution)/shard_map/psum | solution.py:136
  178.8 42.7 %psum.31 = f32[]{:T(128)} all-reduce(f32[]{:T(128)} %psum.30), channel_id=1, replica_groups=mesh['task'=16,'shard'=2] {'task'}, use_global_device_ids=true, to_apply=%region_11.12 | all-reduce | flops 1 | bytes 8 | tf_op jit(solution)/shard_map/psum | solution.py:136
  (68 shorter events, 14.7 us)
Async XLA Ops:
  8.0 3.6 %copy-start.11 = (bf16[1,1024,768]{2,1,0:T(8,128)(2,1)S(1)}, bf16[1,1024,768]{2,1,0:T(8,128)(2,1)}, u32[]{:S(2)}) copy-start(bf16[1,1024,768]{2,1,0:T(8,128)(2,1)} %param.20) | copy-start | bytes 4718596
  8.0 32.3 %all-reduce.2.cloned.1.call-start = ((), (), s32[]{:S(2)}) async-start(), calls=%async_computation.1 | async-start | bytes 4194304 | tf_op jit(solution)/shard_map/psum | solution.py:95
  11.6 2.2 copy-start.20
  11.6 2.2 copy-start.4
  16.2 81.5 %all-gather.2.cloned.1.call-start = ((), (), s32[]{:S(2)}) async-start(), calls=%async_computation.2 | async-start | bytes 4456448 | tf_op jit(solution)/shard_map/all_gather | solution.py:110
  16.7 5.1 %copy-start.15 = (f32[3,4]{1,0:T(4,128)S(1)}, f32[3,4]{1,0:T(4,128)}, u32[]{:S(2)}) copy-start(f32[3,4]{1,0:T(4,128)} %param.29) | copy-start | bytes 148
  16.8 155.2 %reduce-scatter.2.cloned.1.call-start = ((), (), s32[]{:S(2)}) async-start(), calls=%async_computation.3 | async-start | bytes 3145728 | tf_op jit(solution)/shard_map/reduce_scatter | solution.py:128
  21.1 5.9 %copy-start.2 = (bf16[1,1024,768]{1,2,0:T(8,128)(2,1)S(1)}, bf16[1,1024,768]{1,2,0:T(8,128)(2,1)}, u32[]{:S(2)}) copy-start(bf16[1,1024,768]{1,2,0:T(8,128)(2,1)} %copy.21) | copy-start | bytes 4718596
  40.3 3.5 %copy-start.6 = (f32[512,1024]{1,0:T(8,128)S(1)}, f32[512,1024]{1,0:T(8,128)}, u32[]{:S(2)}) copy-start(f32[512,1024]{1,0:T(8,128)} %all-reduce.2.cloned.1.call-done) | copy-start | bytes 6291460
  40.3 3.5 %copy-start.8 = (bf16[1,512,1024]{2,1,0:T(8,128)(2,1)S(1)}, bf16[1,512,1024]{2,1,0:T(8,128)(2,1)}, u32[]{:S(2)}) copy-start(bf16[1,512,1024]{2,1,0:T(8,128)(2,1)} %param.16) | copy-start | bytes 3145732
  43.9 3.4 %copy-start.21 = (f32[512,768]{1,0:T(8,128)S(1)}, f32[512,768]{1,0:T(8,128)}, u32[]{:S(2)}) copy-start(f32[512,768]{1,0:T(8,128)} %copy-done.20) | copy-start | bytes 4718596
  47.2 3.4 %copy-start.22 = (f32[512,768]{1,0:T(8,128)S(1)}, f32[512,768]{1,0:T(8,128)}, u32[]{:S(2)}) copy-start(f32[512,768]{1,0:T(8,128)} %get-tuple-element.58) | copy-start | bytes 4718596
  50.7 13.6 %copy-start.14 = (f32[3,2048]{1,0:T(4,128)S(1)}, f32[3,2048]{1,0:T(4,128)}, u32[]{:S(2)}) copy-start(f32[3,2048]{1,0:T(4,128)} %param.26) | copy-start | bytes 73732
  50.7 46.9 %copy-start.17 = (f32[1,3,512]{2,0,1:T(1,128)S(1)}, f32[1,3,512]{2,0,1:T(1,128)}, u32[]{:S(2)}) copy-start(f32[1,3,512]{2,0,1:T(1,128)} %param.23) | copy-start | bytes 18436
  50.7 46.9 %copy-start.18 = (f32[2048]{0:T(1024)S(1)}, f32[2048]{0:T(1024)}, u32[]{:S(2)}) copy-start(f32[2048]{0:T(1024)} %param.27) | copy-start | bytes 24580
  54.3 47.8 %copy-start.19 = (f32[1,3,512]{2,0,1:T(1,128)S(1)}, f32[1,3,512]{2,0,1:T(1,128)}, u32[]{:S(2)}) copy-start(f32[1,3,512]{2,0,1:T(1,128)} %param.24) | copy-start | bytes 18436
  54.3 47.8 %copy-start.16 = (f32[512,5]{0,1:T(8,128)S(1)}, f32[512,5]{0,1:T(8,128)}, u32[]{:S(2)}) copy-start(f32[512,5]{0,1:T(8,128)} %param.28) | copy-start | bytes 30724
  97.6 7.4 %copy-start.10 = (f32[768,1024]{1,0:T(8,128)S(1)}, f32[768,1024]{1,0:T(8,128)}, u32[]{:S(2)}) copy-start(f32[768,1024]{1,0:T(8,128)} %get-tuple-element.62) | copy-start | bytes 9437188
  105.1 15.3 %copy-start.12 = (bf16[1,512,1024]{2,1,0:T(8,128)(2,1)S(1)}, bf16[1,512,1024]{2,1,0:T(8,128)(2,1)}, u32[]{:S(2)}) copy-start(bf16[1,512,1024]{2,1,0:T(8,128)(2,1)} %param.17) | copy-start | bytes 3145732
  120.4 2.3 copy-start.1
  120.4 2.9 %copy-start.5 = (bf16[1,768,1024]{2,1,0:T(8,128)(2,1)S(1)}, bf16[1,768,1024]{2,1,0:T(8,128)(2,1)}, u32[]{:S(2)}) copy-start(bf16[1,768,1024]{2,1,0:T(8,128)(2,1)} %param.21) | copy-start | bytes 4718596
  123.3 16.4 %copy-start.3 = (bf16[1,1024,768]{1,2,0:T(8,128)(2,1)S(1)}, bf16[1,1024,768]{1,2,0:T(8,128)(2,1)}, u32[]{:S(2)}) copy-start(bf16[1,1024,768]{1,2,0:T(8,128)(2,1)} %copy.21) | copy-start | bytes 4718596
  123.3 16.4 %copy-start.9 = (f32[768,1024]{1,0:T(8,128)S(1)}, f32[768,1024]{1,0:T(8,128)}, u32[]{:S(2)}) copy-start(f32[768,1024]{1,0:T(8,128)} %get-tuple-element.64) | copy-start | bytes 9437188
  166.5 5.4 %copy-start.13 = (bf16[1,512,1024]{2,1,0:T(8,128)(2,1)S(1)}, bf16[1,512,1024]{2,1,0:T(8,128)(2,1)}, u32[]{:S(2)}) copy-start(bf16[1,512,1024]{2,1,0:T(8,128)(2,1)} %param.18) | copy-start | bytes 3145732
  (2 other events, 2.6 us)
Sparse Core Ops, SparseCore 0:
  16.3 24.0 all-reduce.1
  163.7 8.2 reduce-scatter.1
Sparse Core Ops, SparseCore 1:
  19.4 78.2 all-gather.1
